TPU v7x, 32 devices: a whole 2x2x4 slice. The times are simulated.
32 devices in a mesh: grp: 8 (over z, y), mem: 4 (over x, core).
Axes of the slice: x: 2, y: 2, z: 4, core: 2. Of those that a mesh axis runs over, the one named last changes fastest.
Arguments:
- codes: bfloat16 [8192, 1024], P(('grp', 'mem')), as said below
- scales: float32 [8192, 8], P(('grp', 'mem')), may hold values from 0.2 to 2
- cluster_id: int32 [8192], P(('grp', 'mem')), may hold values from 0 to 63, as said below
Outputs:
- smoothed: bfloat16 [8192, 1024], P(('grp', 'mem'))
- dup_mass: bfloat16 [8192], P(('grp', 'mem'))
Inputs may be any that keep to these rules, and one draw needn't show every extreme that they name: `cluster_id`: cluster c belongs to owner group c mod 8. Among the 256 documents of one device, at most 40 belong to clusters of any one owner group, and at most 20 to any one cluster; for each index along mem, some owner group gets exactly 40 from every device of that index, and some cluster of that group exactly 20 from every device of that index. `codes`: documents of one cluster lie near a common direction.
All inputs are finite; a program needn't handle non-finite values.
Results may differ from a plain program's by a relative error of at most 0.0034.
Values may be sent and summed in bfloat16 or wider, within the bound.
No kernel may reach another device: no remote copies, remote signals or barrier semaphores. Data moves between devices by JAX's collectives and lax.ppermute only.
A program may use at most 64 MiB of HBM per device.

v0:
```python
import jax
import jax.numpy as jnp
from jax import lax
from jax.sharding import PartitionSpec as P

CAP = 40


def embed(codes, scales):
    rows, width = codes.shape
    nblk = scales.shape[1]
    x = (codes.astype(jnp.float32).reshape(rows, nblk, width // nblk) * scales[:, :, None]).reshape(
        rows, width
    )
    inv = lax.rsqrt(jnp.mean(x * x, axis=1, keepdims=True) + 1e-06)
    return (x * inv).astype(jnp.bfloat16)


def make_fold(queries, qtags, query_index):
    width = queries.shape[1]

    def accumulate(carry, piece, start):
        keys, ktags = piece
        member_count = keys.shape[0]
        sims = (
            lax.dot_general(
                queries, keys, (((1,), (1,)), ((), ())), preferred_element_type=jnp.float32
            )
            / width
        )
        key_index = jnp.arange(member_count, dtype=jnp.int32)
        keep = (
            (qtags[:, None] == ktags[None, :])
            & (qtags[:, None] >= 0)
            & (query_index[:, None] != key_index[None, :])
        )
        weights = jnp.where(keep, jnp.exp(8.0 * (sims - 1.0)), jnp.float32(0.0))
        den_sum = jnp.sum(weights, axis=1)
        numerator_sum = jnp.dot(
            weights.astype(jnp.bfloat16), keys, preferred_element_type=jnp.float32
        )
        return (den_sum, numerator_sum)

    return accumulate


def local(codes, scales, cluster_id):
    rows, width = codes.shape
    groups = lax.axis_size("grp")
    member = lax.axis_index("mem")
    embedding_rows = embed(codes, scales)
    owner = cluster_id % groups
    onehot = (owner[:, None] == jnp.arange(groups, dtype=jnp.int32)[None, :]).astype(jnp.int32)
    ranks = jnp.cumsum(onehot, axis=0) - 1
    slot = jnp.sum(ranks * onehot, axis=1)
    target = owner * CAP + slot
    outbox = (
        jnp.zeros((groups * CAP, width), jnp.bfloat16)
        .at[target]
        .set(embedding_rows)
        .reshape(groups, CAP, width)
    )
    outtags = (
        jnp.full((groups * CAP,), -1.0, jnp.float32)
        .at[target]
        .set(cluster_id.astype(jnp.float32))
        .astype(jnp.bfloat16)
        .reshape(groups, CAP)
    )
    slots = groups * CAP
    inbox, incoming_tags = (
        lax.all_to_all(outbox, "grp", split_axis=0, concat_axis=0, tiled=True),
        lax.all_to_all(outtags, "grp", split_axis=0, concat_axis=0, tiled=True),
    )
    queries = inbox.reshape(slots, width)
    qtags = incoming_tags.reshape(slots)
    start_carry = (jnp.zeros((slots,), jnp.float32), jnp.zeros((slots, width), jnp.float32))
    query_index = member * slots + jnp.arange(slots, dtype=jnp.int32)
    accumulate = make_fold(queries, qtags, query_index)
    den_sum, numerator_sum = accumulate(
        start_carry,
        (
            lax.all_gather(queries, "mem", axis=0, tiled=True),
            lax.all_gather(qtags, "mem", axis=0, tiled=True),
        ),
        jnp.int32(0),
    )
    den = 1.0 + den_sum
    result = ((queries.astype(jnp.float32) + numerator_sum) / den[:, None]).astype(jnp.bfloat16)
    mass = jnp.log(den).astype(jnp.bfloat16)
    back_rows, back_mass = (
        lax.all_to_all(
            result.reshape(groups, CAP, width), "grp", split_axis=0, concat_axis=0, tiled=True
        ),
        lax.all_to_all(mass.reshape(groups, CAP), "grp", split_axis=0, concat_axis=0, tiled=True),
    )
    smoothed = back_rows.reshape(slots, width)[target]
    dup_mass = back_mass.reshape(slots)[target]
    return (smoothed, dup_mass)


def solution(mesh):
    placed = (P(("grp", "mem"), None), P(("grp", "mem"), None), P(("grp", "mem")))
    return jax.shard_map(
        local,
        mesh=mesh,
        in_specs=placed,
        out_specs=(P(("grp", "mem"), None), P(("grp", "mem"))),
        check_vma=False,
    )
```

profile of v0, /device:TPU:0, one launch (start us, length us, event | category | flops | bytes accessed | tf_op | source)
XLA Modules:
  0.0 107.8 jit_solution(3126384838830802530)
XLA Ops:
  7.2 0.0 copy-start.1
  7.2 0.0 all-gather.2.cloned.1.call-start
  7.2 0.8 fusion.14
  8.0 0.6 reduce-window.6
  8.6 0.2 slice_reduce_fusion
  8.8 0.1 fusion.9
  8.9 0.8 copy.7
  9.8 0.3 mul.43
  10.1 0.0 copy-done.1
  10.1 0.3 multiply_reduce_fusion
  10.4 0.0 copy-start.3
  10.4 2.0 %scatter_custom_fusion = bf16[320,1024]{1,0:T(8,128)(2,1)S(1)} fusion(s32[256]{0:T(256)S(1)} %compare_select_fusion, f32[32,8,8,128]{3,2,1,0:T(8,128)S(1)} %bitcast.26, bf16[256,1024]{1,0:T(8,128)(2,1)S(1)} %copy-done.1, f32[256]{0:T(256)S(1)} %add_rsqrt_fusion, bf16[]{:T(256)} %constant.16.clone.1), kind=kCustom, calls=%fused_computation.17 | custom fusion | flops 1048576 | bytes 2229250 | tf_op jit(solution)/shard_map/scatter | solution.py:60
  12.4 24.9 %all_to_all.26 = bf16[8,40,1024]{2,1,0:T(8,128)(2,1)} all-to-all(bf16[8,40,1024]{2,1,0:T(8,128)(2,1)S(1)} %bitcast.30), channel_id=1, replica_groups=mesh['grp'=8,'mem'=4] {'grp'}, dimensions={0} | all-to-all | bytes 1310720 | tf_op jit(solution)/shard_map/all_to_all | solution.py:72
  37.3 0.0 all-gather.2.cloned.1.call-update
  37.3 1.4 %scatter_custom_fusion.1 = f32[320]{0:T(512)S(1)} fusion(s32[256]{0:T(256)S(1)} %compare_select_fusion, f32[256]{0:T(256)S(1)} %get-tuple-element.4, f32[]{:T(128)} %constant.49.clone.1), kind=kCustom, calls=%fused_computation.35 | custom fusion | bytes 1284 | tf_op jit(solution)/shard_map/scatter | solution.py:66
  38.7 0.7 all_to_all.21
  39.4 3.3 %all-to-all-start.1 = ((bf16[8,1,40]{2,1,0:T(2,128)(2,1)}), bf16[8,1,40]{2,1,0:T(2,128)(2,1)S(1)}, u32[]{:S(2)}, u32[]{:S(2)}) async-start(bf16[8,1,40]{2,1,0:T(2,128)(2,1)} %all_to_all.21), calls=%async_computation.1 | async-start | bytes 8192 | tf_op jit(solution)/shard_map/all_to_all | solution.py:73
  42.8 0.0 copy-done.3
  42.8 0.6 dynamic-slice
  44.0 5.1 %all-to-all-done.1 = bf16[8,1,40]{2,1,0:T(2,128)(2,1)S(1)} async-done(((bf16[8,1,40]{2,1,0:T(2,128)(2,1)}), bf16[8,1,40]{2,1,0:T(2,128)(2,1)S(1)}, u32[]{:S(2)}, u32[]{:S(2)}) %all-to-all-start.1) | async-done | bytes 672 | tf_op jit(solution)/shard_map/all_to_all | solution.py:73
  49.1 0.1 reshape.140
  49.2 0.3 dynamic-update-slice
  49.4 6.1 %all-reduce = bf16[1280]{0:T(1024)(128)(2,1)S(1)} all-reduce(bf16[1280]{0:T(1024)(128)(2,1)S(1)} %dynamic-update-slice), channel_id=1, replica_groups=mesh['grp'=8,'mem'=4] {'mem'}, use_global_device_ids=true, to_apply=%add | all-reduce | flops 1280 | bytes 5120
  55.6 0.0 copy-start
  55.6 6.2 %all-gather.2.cloned.1.call-done = bf16[1280,1024]{1,0:T(8,128)(2,1)} async-done(((bf16[320,1024]{1,0:T(8,128)(2,1)}), bf16[1280,1024]{1,0:T(8,128)(2,1)}) %all-gather.2.cloned.1.call-update) | async-done | bytes 2621456 | tf_op jit(solution)/shard_map/all_gather | solution.py:83
  61.8 0.0 copy-start.2
  61.8 4.5 %fusion.15 = (f32[320]{0:T(512)S(1)}, bf16[320,1280]{1,0:T(8,128)(2,1)}) fusion(bf16[320,1024]{1,0:T(8,128)(2,1)} %bitcast.28, bf16[1280,1024]{1,0:T(8,128)(2,1)} %all-gather.2.cloned.1.call-done, s32[320]{0:T(512)S(1)} %iota_add_fusion, pred[320]{0:T(512)(128)(4,1)S(1)} %broadcast_compare_fusion, bf16[1280]{0:T(1024)(128)(2,1)S(1)} %all-reduce, ...), kind=kOutput, calls=%fused_computation.40 | convolution fusion | flops 843775680 | bytes 4102080 | tf_op jit(solution)/shard_map/dot_general | solution.py:26
  66.3 0.7 convert_element_type.50
  67.0 5.5 %all-to-all-start.3 = ((bf16[8,1,40]{2,1,0:T(2,128)(2,1)}), bf16[8,1,40]{2,1,0:T(2,128)(2,1)S(1)}, u32[]{:S(2)}, u32[]{:S(2)}) async-start(bf16[8,1,40]{2,1,0:T(2,128)(2,1)} %convert_element_type.50), calls=%async_computation.3 | async-start | bytes 8192 | tf_op jit(solution)/shard_map/all_to_all | solution.py:95
  72.5 0.0 copy-done
  72.5 0.0 copy-done.2
  72.5 3.1 %divide_convert_fusion = bf16[320,1024]{1,0:T(8,128)(2,1)} fusion(bf16[1280,1024]{1,0:T(8,128)(2,1)S(1)} %copy-done.2, bf16[320,1024]{1,0:T(8,128)(2,1)S(1)} %bitcast.29, bf16[320,1280]{1,0:T(8,128)(2,1)} %get-tuple-element.7, f32[320]{0:T(512)S(1)} %get-tuple-element.3), kind=kOutput, calls=%fused_computation.12 | convolution fusion | flops 840171520 | bytes 4752640 | tf_op jit(solution)/shard_map/dot_general | solution.py:39
  75.6 3.3 %all-to-all-done.3 = bf16[8,1,40]{2,1,0:T(2,128)(2,1)S(1)} async-done(((bf16[8,1,40]{2,1,0:T(2,128)(2,1)}), bf16[8,1,40]{2,1,0:T(2,128)(2,1)S(1)}, u32[]{:S(2)}, u32[]{:S(2)}) %all-to-all-start.3) | async-done | bytes 672 | tf_op jit(solution)/shard_map/all_to_all | solution.py:95
  78.9 3.5 %all-to-all-start.2 = ((bf16[8,40,1024]{2,1,0:T(8,128)(2,1)}), bf16[8,40,1024]{2,1,0:T(8,128)(2,1)S(1)}, u32[]{:S(2)}, u32[]{:S(2)}) async-start(bf16[8,40,1024]{2,1,0:T(8,128)(2,1)} %bitcast.6), calls=%async_computation.2 | async-start | bytes 1310720 | tf_op jit(solution)/shard_map/all_to_all | solution.py:92
  82.5 0.1 reshape.103
  82.6 2.5 %gather_fusion.1 = bf16[256]{0:T(256)(128)(2,1)} fusion(bf16[320]{0:T(512)(128)(2,1)S(1)} %reshape.103, s32[1024]{0:T(1024)S(1)} %pad_clamp_fusion), kind=kCustom, calls=%fused_computation.1 | custom fusion | bytes 2048 | tf_op jit(solution)/shard_map/gather | solution.py:98
  85.0 13.9 %all-to-all-done.2 = bf16[8,40,1024]{2,1,0:T(8,128)(2,1)S(1)} async-done(((bf16[8,40,1024]{2,1,0:T(8,128)(2,1)}), bf16[8,40,1024]{2,1,0:T(8,128)(2,1)S(1)}, u32[]{:S(2)}, u32[]{:S(2)}) %all-to-all-start.2) | async-done | bytes 655392 | tf_op jit(solution)/shard_map/all_to_all | solution.py:92
  98.9 2.0 %gather_fusion = bf16[256,1024]{1,0:T(8,128)(2,1)} fusion(bf16[320,1024]{1,0:T(8,128)(2,1)S(1)} %bitcast.24, s32[1024]{0:T(1024)S(1)} %pad_clamp_fusion), kind=kCustom, calls=%fused_computation | custom fusion | bytes 1049600 | tf_op jit(solution)/shard_map/gather | solution.py:97
  (13 shorter events, 0.1 us)
Async XLA Ops:
  7.2 2.9 %copy-start.1 = (bf16[256,1024]{1,0:T(8,128)(2,1)S(1)}, bf16[256,1024]{1,0:T(8,128)(2,1)}, u32[]{:S(2)}) copy-start(bf16[256,1024]{1,0:T(8,128)(2,1)} %param.3) | copy-start | bytes 1572868
  7.2 54.6 %all-gather.2.cloned.1.call-start = ((), (), s32[]{:S(2)}) async-start(), calls=%async_computation.4 | async-start | bytes 3276800 | tf_op jit(solution)/shard_map/all_gather | solution.py:83
  10.4 32.4 %copy-start.3 = (u32[32]{0:T(128)S(1)}, u32[32]{0:T(128)}, u32[]{:S(2)}) copy-start(u32[32]{0:T(128)} %constant.55) | copy-start | bytes 388
  39.4 9.6 %all-to-all-start.1 = ((bf16[8,1,40]{2,1,0:T(2,128)(2,1)}), bf16[8,1,40]{2,1,0:T(2,128)(2,1)S(1)}, u32[]{:S(2)}, u32[]{:S(2)}) async-start(bf16[8,1,40]{2,1,0:T(2,128)(2,1)} %all_to_all.21), calls=%async_computation.1 | async-start | bytes 8192 | tf_op jit(solution)/shard_map/all_to_all | solution.py:73
  55.6 16.9 %copy-start = (bf16[8,40,1024]{2,1,0:T(8,128)(2,1)S(1)}, bf16[8,40,1024]{2,1,0:T(8,128)(2,1)}, u32[]{:S(2)}) copy-start(bf16[8,40,1024]{2,1,0:T(8,128)(2,1)} %all_to_all.26) | copy-start | bytes 1966084
  61.8 10.7 %copy-start.2 = (bf16[1280,1024]{1,0:T(8,128)(2,1)S(1)}, bf16[1280,1024]{1,0:T(8,128)(2,1)}, u32[]{:S(2)}) copy-start(bf16[1280,1024]{1,0:T(8,128)(2,1)} %all-gather.2.cloned.1.call-done) | copy-start | bytes 7864324
  67.0 11.9 %all-to-all-start.3 = ((bf16[8,1,40]{2,1,0:T(2,128)(2,1)}), bf16[8,1,40]{2,1,0:T(2,128)(2,1)S(1)}, u32[]{:S(2)}, u32[]{:S(2)}) async-start(bf16[8,1,40]{2,1,0:T(2,128)(2,1)} %convert_element_type.50), calls=%async_computation.3 | async-start | bytes 8192 | tf_op jit(solution)/shard_map/all_to_all | solution.py:95
  78.9 20.1 %all-to-all-start.2 = ((bf16[8,40,1024]{2,1,0:T(8,128)(2,1)}), bf16[8,40,1024]{2,1,0:T(8,128)(2,1)S(1)}, u32[]{:S(2)}, u32[]{:S(2)}) async-start(bf16[8,40,1024]{2,1,0:T(8,128)(2,1)} %bitcast.6), calls=%async_computation.2 | async-start | bytes 1310720 | tf_op jit(solution)/shard_map/all_to_all | solution.py:92
Sparse Core Ops, SparseCore 0:
  37.4 24.3 all-gather.1
where the time goes:
time: 108 us
  blocking collectives  31 us (29%)
  waiting for transfers between devices  28.5 us (26%)
  between operations  14.8 us (14%)
  starting transfers between devices  12.4 us (11%)
  local copies, waits for them, and re-layouts  9.58 us (9%)
  matrix products  7.54 us (7%)
  other arithmetic  3.82 us (4%)
    all_to_all x1, blocking collectives, local(): lax.all_to_all(outbox, 'grp', split_axis=0, concat_axis=0, tiled=True)  24.9 us
    all_to_all x1, waiting for transfers between devices, local(): lax.all_to_all(result.reshape(groups, CAP, width), 'grp', split_axis=0, c...  13.9 us
    all_gather x1, waiting for transfers between devices, local(): lax.all_gather(queries, 'mem', axis=0, tiled=True)  6.2 us
    unnamed x1, blocking collectives  6.14 us
    all_to_all x1, starting transfers between devices, local(): lax.all_to_all(mass.reshape(groups, CAP), 'grp', split_axis=0, concat_axi...  5.52 us
    all_to_all x1, waiting for transfers between devices, local(): lax.all_to_all(outtags, 'grp', split_axis=0, concat_axis=0, tiled=True)  5.05 us
    dot_general x1, matrix products, accumulate(): lax.dot_general(queries, keys, (((1,), (1,)), ((), ())), preferred_elemen...  4.49 us
    all_to_all x1, starting transfers between devices, local(): lax.all_to_all(result.reshape(groups, CAP, width), 'grp', split_axis=0, c...  3.54 us
  transfers between devices with their start and end apart: 4, of which 4 were waited for; matrix products, arithmetic and copies ran while one was open for 7% of the time, Pallas kernels for 0%

commit v1 on v0

--- a/solution.py
+++ b/solution.py
@@ -2,8 +2,15 @@
 import jax.numpy as jnp
 from jax import lax
 from jax.sharding import PartitionSpec as P
+from jax.lax import all_to_all, axis_size
 
 CAP = 40
+
+
+def detail_gates_on_mesh(vec):
+    world = axis_size("mem")
+    pieces_in = tuple((world if idx == 0 else 1 for idx in range(vec.ndim)))
+    return all_to_all(jnp.tile(vec, pieces_in), "mem", tiled=True, split_axis=0, concat_axis=0)
 
 
 def embed(codes, scales):
@@ -79,10 +86,7 @@
     accumulate = make_fold(queries, qtags, query_index)
     den_sum, numerator_sum = accumulate(
         start_carry,
-        (
-            lax.all_gather(queries, "mem", axis=0, tiled=True),
-            lax.all_gather(qtags, "mem", axis=0, tiled=True),
-        ),
+        (detail_gates_on_mesh(queries), lax.all_gather(qtags, "mem", axis=0, tiled=True)),
         jnp.int32(0),
     )
     den = 1.0 + den_sum

time: 108 us -> 111 us (1.028)
  blocking collectives: 31 us -> 51.1 us
  between operations: 14.8 us -> 1.43 us
  waiting for transfers between devices: 28.5 us -> 19.7 us
  starting transfers between devices: 12.4 us -> 17.9 us
  matrix products: 7.54 us -> 5.48 us
  local copies, waits for them, and re-layouts: 9.58 us -> 11.4 us
    unnamed x1, blocking collectives: 6.14 us -> 31.1 us
    all_gather x1 -> x0, waiting for transfers between devices: 6.2 us -> none  [local(): lax.all_gather(queries, 'mem', axis=0, tiled=True)]
    all_to_all x1, blocking collectives: 24.9 us -> 20 us  [local(): lax.all_to_all(outbox, 'grp', split_axis=0, concat_axis=0, tiled=True)]
    all_to_all x1, starting transfers between devices: 3.31 us -> 7.28 us  [local(): lax.all_to_all(outtags, 'grp', split_axis=0, concat_axis=0, tiled=True)]
    all_to_all x0 -> x1, starting transfers between devices: none -> 3.78 us  [detail_gates_on_mesh(): all_to_all(jnp.tile(vec, pieces_in), 'mem', tiled=True, split_axis=0, con...]
    all_to_all x1, starting transfers between devices: 5.52 us -> 3.31 us  [local(): lax.all_to_all(mass.reshape(groups, CAP), 'grp', split_axis=0, concat_axi...]
    all_to_all x1, waiting for transfers between devices: 5.05 us -> 2.95 us  [local(): lax.all_to_all(outtags, 'grp', split_axis=0, concat_axis=0, tiled=True)]
    dot_general x1, matrix products: 4.49 us -> 2.43 us  [accumulate(): lax.dot_general(queries, keys, (((1,), (1,)), ((), ())), preferred_elemen...]
  transfers between devices with their start and end apart: 4 -> 4, of which waited for: 4 -> 3; matrix products, arithmetic and copies ran while one was open for 7% -> 9% of each run, Pallas kernels for 0% -> 0%
where the time goes in v1:
time: 111 us
  blocking collectives  51.1 us (46%)
  waiting for transfers between devices  19.7 us (18%)
  starting transfers between devices  17.9 us (16%)
  local copies, waits for them, and re-layouts  11.4 us (10%)
  matrix products  5.48 us (5%)
  other arithmetic  3.83 us (3%)
  between operations  1.43 us (1%)
    unnamed x1, blocking collectives  31.1 us
    all_to_all x1, blocking collectives, local(): lax.all_to_all(outbox, 'grp', split_axis=0, concat_axis=0, tiled=True)  20 us
    all_to_all x1, waiting for transfers between devices, local(): lax.all_to_all(result.reshape(groups, CAP, width), 'grp', split_axis=0, c...  13.5 us
    all_to_all x1, starting transfers between devices, local(): lax.all_to_all(outtags, 'grp', split_axis=0, concat_axis=0, tiled=True)  7.28 us
    all_to_all x1, starting transfers between devices, detail_gates_on_mesh(): all_to_all(jnp.tile(vec, pieces_in), 'mem', tiled=True, split_axis=0, con...  3.78 us
    all_to_all x1, starting transfers between devices, local(): lax.all_to_all(result.reshape(groups, CAP, width), 'grp', split_axis=0, c...  3.54 us
    all_to_all x1, starting transfers between devices, local(): lax.all_to_all(mass.reshape(groups, CAP), 'grp', split_axis=0, concat_axi...  3.31 us
    all_to_all x1, waiting for transfers between devices, local(): lax.all_to_all(mass.reshape(groups, CAP), 'grp', split_axis=0, concat_axi...  3.28 us
  transfers between devices with their start and end apart: 4, of which 3 were waited for; matrix products, arithmetic and copies ran while one was open for 9% of the time, Pallas kernels for 0%

profile of v1, /device:TPU:0, one launch (start us, length us, event | category | flops | bytes accessed | tf_op | source)
XLA Modules:
  0.0 110.9 jit_solution(17379971462033012531)
XLA Ops:
  0.6 0.0 copy-start
  0.6 0.8 fusion.14
  1.4 0.6 reduce-window.6
  2.0 0.2 slice_reduce_fusion
  2.2 0.1 fusion.9
  2.4 1.4 %scatter_custom_fusion.1 = f32[320]{0:T(512)S(1)} fusion(s32[256]{0:T(256)S(1)} %compare_select_fusion, f32[256]{0:T(256)S(1)} %get-tuple-element.4, f32[]{:T(128)} %constant.49.clone.1), kind=kCustom, calls=%fused_computation.35 | custom fusion | bytes 1284 | tf_op jit(solution)/shard_map/scatter | solution.py:73
  3.8 0.7 all_to_all.29
  4.5 7.3 %all-to-all-start.1 = ((bf16[8,1,40]{2,1,0:T(2,128)(2,1)}), bf16[8,1,40]{2,1,0:T(2,128)(2,1)S(1)}, u32[]{:S(2)}, u32[]{:S(2)}) async-start(bf16[8,1,40]{2,1,0:T(2,128)(2,1)} %all_to_all.29), calls=%async_computation.1 | async-start | bytes 8192 | tf_op jit(solution)/shard_map/all_to_all | solution.py:80
  11.7 0.8 copy.7
  12.6 0.3 mul.43
  12.9 0.0 copy-done
  12.9 0.3 multiply_reduce_fusion
  13.2 2.0 %scatter_custom_fusion = bf16[320,1024]{1,0:T(8,128)(2,1)S(1)} fusion(s32[256]{0:T(256)S(1)} %compare_select_fusion, f32[32,8,8,128]{3,2,1,0:T(8,128)S(1)} %bitcast.27, bf16[256,1024]{1,0:T(8,128)(2,1)S(1)} %copy-done, f32[256]{0:T(256)S(1)} %add_rsqrt_fusion, bf16[]{:T(256)} %constant.16.clone.1), kind=kCustom, calls=%fused_computation.17 | custom fusion | flops 1048576 | bytes 2229250 | tf_op jit(solution)/shard_map/scatter | solution.py:67
  15.2 2.9 %all-to-all-done.1 = bf16[8,1,40]{2,1,0:T(2,128)(2,1)S(1)} async-done(((bf16[8,1,40]{2,1,0:T(2,128)(2,1)}), bf16[8,1,40]{2,1,0:T(2,128)(2,1)S(1)}, u32[]{:S(2)}, u32[]{:S(2)}) %all-to-all-start.1) | async-done | bytes 672 | tf_op jit(solution)/shard_map/all_to_all | solution.py:80
  18.1 20.0 %all_to_all.35 = bf16[8,40,1024]{2,1,0:T(8,128)(2,1)S(1)} all-to-all(bf16[8,40,1024]{2,1,0:T(8,128)(2,1)S(1)} %bitcast.33), channel_id=1, replica_groups=mesh['grp'=8,'mem'=4] {'grp'}, dimensions={0} | all-to-all | bytes 1310720 | tf_op jit(solution)/shard_map/all_to_all | solution.py:79
  38.1 1.8 %tile.2 = bf16[4,320,1024]{2,1,0:T(8,128)(2,1)} broadcast(bf16[320,1024]{1,0:T(8,128)(2,1)S(1)} %bitcast.30), dimensions={1,2} | broadcast | bytes 3276800 | tf_op jit(solution)/shard_map/tile | solution.py:13
  40.0 0.0 copy-start.1
  40.0 3.8 %all-to-all-start.2 = ((bf16[4,320,1024]{2,1,0:T(8,128)(2,1)}), bf16[4,320,1024]{2,1,0:T(8,128)(2,1)S(1)}, u32[]{:S(2)}, u32[]{:S(2)}) async-start(bf16[4,320,1024]{2,1,0:T(8,128)(2,1)} %tile.2), calls=%async_computation.2 | async-start | bytes 5242880 | tf_op jit(solution)/shard_map/all_to_all | solution.py:13
  43.8 0.0 copy-done.1
  43.8 0.6 dynamic-slice
  45.1 0.1 reshape.147
  45.2 0.3 dynamic-update-slice
  45.4 31.1 %all-reduce = bf16[1280]{0:T(1024)(128)(2,1)S(1)} all-reduce(bf16[1280]{0:T(1024)(128)(2,1)S(1)} %dynamic-update-slice), channel_id=1, replica_groups=mesh['grp'=8,'mem'=4] {'mem'}, use_global_device_ids=true, to_apply=%add | all-reduce | flops 1280 | bytes 5120
  76.5 0.0 all-to-all-done.2
  76.5 2.4 %fusion.15 = (f32[320]{0:T(512)S(1)}, bf16[320,1280]{1,0:T(8,128)(2,1)}) fusion(bf16[320,1024]{1,0:T(8,128)(2,1)S(1)} %bitcast.31, bf16[1280,1024]{1,0:T(8,128)(2,1)S(1)} %bitcast.28, s32[320]{0:T(512)S(1)} %iota_add_fusion, pred[320]{0:T(512)(128)(4,1)S(1)} %broadcast_compare_fusion, bf16[1280]{0:T(1024)(128)(2,1)S(1)} %all-reduce, ...), kind=kOutput, calls=%fused_computation.40 | convolution fusion | flops 843775680 | bytes 4102080 | tf_op jit(solution)/shard_map/dot_general | solution.py:33
  79.0 0.7 convert_element_type.50
  79.6 3.3 %all-to-all-start.4 = ((bf16[8,1,40]{2,1,0:T(2,128)(2,1)}), bf16[8,1,40]{2,1,0:T(2,128)(2,1)S(1)}, u32[]{:S(2)}, u32[]{:S(2)}) async-start(bf16[8,1,40]{2,1,0:T(2,128)(2,1)} %convert_element_type.50), calls=%async_computation.4 | async-start | bytes 8192 | tf_op jit(solution)/shard_map/all_to_all | solution.py:99
  83.0 3.0 %divide_convert_fusion = bf16[320,1024]{1,0:T(8,128)(2,1)} fusion(bf16[1280,1024]{1,0:T(8,128)(2,1)S(1)} %bitcast.29, bf16[320,1024]{1,0:T(8,128)(2,1)S(1)} %bitcast.32, bf16[320,1280]{1,0:T(8,128)(2,1)} %get-tuple-element.7, f32[320]{0:T(512)S(1)} %get-tuple-element.3), kind=kOutput, calls=%fused_computation.12 | convolution fusion | flops 840171520 | bytes 4752640 | tf_op jit(solution)/shard_map/dot_general | solution.py:46
  86.0 3.3 %all-to-all-done.4 = bf16[8,1,40]{2,1,0:T(2,128)(2,1)S(1)} async-done(((bf16[8,1,40]{2,1,0:T(2,128)(2,1)}), bf16[8,1,40]{2,1,0:T(2,128)(2,1)S(1)}, u32[]{:S(2)}, u32[]{:S(2)}) %all-to-all-start.4) | async-done | bytes 672 | tf_op jit(solution)/shard_map/all_to_all | solution.py:99
  89.3 3.5 %all-to-all-start.3 = ((bf16[8,40,1024]{2,1,0:T(8,128)(2,1)}), bf16[8,40,1024]{2,1,0:T(8,128)(2,1)S(1)}, u32[]{:S(2)}, u32[]{:S(2)}) async-start(bf16[8,40,1024]{2,1,0:T(8,128)(2,1)} %bitcast.34), calls=%async_computation.3 | async-start | bytes 1310720 | tf_op jit(solution)/shard_map/all_to_all | solution.py:96
  92.9 0.1 reshape.110
  93.0 2.5 %gather_fusion.1 = bf16[256]{0:T(256)(128)(2,1)} fusion(bf16[320]{0:T(512)(128)(2,1)S(1)} %reshape.110, s32[1024]{0:T(1024)S(1)} %pad_clamp_fusion), kind=kCustom, calls=%fused_computation.1 | custom fusion | bytes 2048 | tf_op jit(solution)/shard_map/gather | solution.py:102
  95.4 13.5 %all-to-all-done.3 = bf16[8,40,1024]{2,1,0:T(8,128)(2,1)S(1)} async-done(((bf16[8,40,1024]{2,1,0:T(8,128)(2,1)}), bf16[8,40,1024]{2,1,0:T(8,128)(2,1)S(1)}, u32[]{:S(2)}, u32[]{:S(2)}) %all-to-all-start.3) | async-done | bytes 655392 | tf_op jit(solution)/shard_map/all_to_all | solution.py:96
  108.9 2.0 %gather_fusion = bf16[256,1024]{1,0:T(8,128)(2,1)} fusion(bf16[320,1024]{1,0:T(8,128)(2,1)S(1)} %bitcast.25, s32[1024]{0:T(1024)S(1)} %pad_clamp_fusion), kind=kCustom, calls=%fused_computation | custom fusion | bytes 1049600 | tf_op jit(solution)/shard_map/gather | solution.py:101
  (13 shorter events, 0.1 us)
Async XLA Ops:
  0.6 12.3 %copy-start = (bf16[256,1024]{1,0:T(8,128)(2,1)S(1)}, bf16[256,1024]{1,0:T(8,128)(2,1)}, u32[]{:S(2)}) copy-start(bf16[256,1024]{1,0:T(8,128)(2,1)} %param.3) | copy-start | bytes 1572868
  4.5 13.7 %all-to-all-start.1 = ((bf16[8,1,40]{2,1,0:T(2,128)(2,1)}), bf16[8,1,40]{2,1,0:T(2,128)(2,1)S(1)}, u32[]{:S(2)}, u32[]{:S(2)}) async-start(bf16[8,1,40]{2,1,0:T(2,128)(2,1)} %all_to_all.29), calls=%async_computation.1 | async-start | bytes 8192 | tf_op jit(solution)/shard_map/all_to_all | solution.py:80
  40.0 3.8 %copy-start.1 = (u32[32]{0:T(128)S(1)}, u32[32]{0:T(128)}, u32[]{:S(2)}) copy-start(u32[32]{0:T(128)} %constant.55) | copy-start | bytes 388
  40.0 36.5 %all-to-all-start.2 = ((bf16[4,320,1024]{2,1,0:T(8,128)(2,1)}), bf16[4,320,1024]{2,1,0:T(8,128)(2,1)S(1)}, u32[]{:S(2)}, u32[]{:S(2)}) async-start(bf16[4,320,1024]{2,1,0:T(8,128)(2,1)} %tile.2), calls=%async_computation.2 | async-start | bytes 5242880 | tf_op jit(solution)/shard_map/all_to_all | solution.py:13
  79.6 9.6 %all-to-all-start.4 = ((bf16[8,1,40]{2,1,0:T(2,128)(2,1)}), bf16[8,1,40]{2,1,0:T(2,128)(2,1)S(1)}, u32[]{:S(2)}, u32[]{:S(2)}) async-start(bf16[8,1,40]{2,1,0:T(2,128)(2,1)} %convert_element_type.50), calls=%async_computation.4 | async-start | bytes 8192 | tf_op jit(solution)/shard_map/all_to_all | solution.py:99
  89.3 19.6 %all-to-all-start.3 = ((bf16[8,40,1024]{2,1,0:T(8,128)(2,1)}), bf16[8,40,1024]{2,1,0:T(8,128)(2,1)S(1)}, u32[]{:S(2)}, u32[]{:S(2)}) async-start(bf16[8,40,1024]{2,1,0:T(8,128)(2,1)} %bitcast.34), calls=%async_computation.3 | async-start | bytes 1310720 | tf_op jit(solution)/shard_map/all_to_all | solution.py:96
